TPU v7x, 32 devices: a whole 2x2x4 slice. The times are simulated.
32 devices in a mesh: blk: 8 (over y, x, core), slab: 4 (over z).
Axes of the slice: x: 2, y: 2, z: 4, core: 2. Of those that a mesh axis runs over, the one named last changes fastest.
Arguments:
- old_factor: bfloat16 [8192, 24576], P('slab', 'blk'), may hold values from -0.0546875 to 0.0546875
- solved: bfloat16 [24576, 256], P('blk', 'slab'), may hold values from -6 to 6
- band: bfloat16 [8192, 8192], P('blk'), may hold values from -0.0625 to 0.0625
- inv_diag: bfloat16 [2048, 8192], P(None, 'blk'), may hold values from -1 to 2, as said below
- rhs: bfloat16 [8192, 256], P('blk', 'slab'), may hold values from -6 to 6
Outputs:
- solution: bfloat16 [8192, 256], P('blk', 'slab')
Inputs may be any that keep to these rules, and one draw needn't show every extreme that they name: `inv_diag`: columns k * 2048 to (k + 1) * 2048 - 1 hold the inverse applied in block step k.
All inputs are finite; a program needn't handle non-finite values.
Results may differ from a plain program's by a relative error of at most 0.008.
Values may be sent and summed in bfloat16 or wider, within the bound.
A program may use at most 64 MiB of HBM per device.

v0:
```python
import jax
import jax.numpy as jnp
from jax import lax
from jax.sharding import PartitionSpec as P

STEPS = 4


def body(old_factor, solved, band, inv_diag, rhs):
    own_rows = rhs.shape[0]
    block_rows = inv_diag.shape[0]
    group_size = block_rows // own_rows
    own_index = lax.axis_index("blk")
    own_block = own_index // group_size
    offset = own_index % group_size * own_rows
    partial_value = jnp.dot(
        old_factor,
        lax.all_gather(solved, "slab", axis=1, tiled=True),
        preferred_element_type=jnp.float32,
    )
    window_terms = lax.all_to_all(partial_value, "slab", split_axis=1, concat_axis=0, tiled=True)
    source = rhs.astype(jnp.float32)
    accum = lax.psum_scatter(window_terms, "blk", scatter_dimension=0, tiled=True)
    solution = jnp.zeros(rhs.shape, jnp.bfloat16)
    for step in range(STEPS):
        total = accum
        resid = (source - total).astype(jnp.bfloat16)
        term = jnp.dot(inv_diag, resid, preferred_element_type=jnp.float32)
        term = jnp.where(own_block == step, term, jnp.zeros_like(term))
        newest = lax.psum(term, "blk").astype(jnp.bfloat16)
        mine = lax.dynamic_slice_in_dim(newest, offset, own_rows, 0)
        solution = jnp.where(own_block == step, mine, solution)
        if step + 1 < STEPS:
            columns = band[:, step * block_rows : (step + 1) * block_rows]
            update = jnp.dot(columns, newest, preferred_element_type=jnp.float32)
            accum = accum + jnp.where(own_block > step, update, jnp.zeros_like(update))
    return solution


def solution(mesh):
    return jax.shard_map(
        body,
        mesh=mesh,
        in_specs=(
            P("slab", "blk"),
            P("blk", "slab"),
            P("blk", None),
            P(None, "blk"),
            P("blk", "slab"),
        ),
        out_specs=P("blk", "slab"),
        check_vma=False,
    )
```

profile of v0, /device:TPU:0, one launch (start us, length us, event | category | flops | bytes accessed | tf_op | source)
XLA Modules:
  0.0 292.5 jit_solution(17000383142873836997)
XLA Ops:
  6.5 0.0 all-gather.2.cloned.1.call-start
  6.5 0.7 all-gather.2.cloned.1.call-update
  7.3 0.0 reduce-scatter.2.cloned.1.call-start
  7.3 41.4 %all-gather.2.cloned.1.call-done = bf16[3072,256]{0,1:T(8,128)(2,1)} async-done(((bf16[3072,64]{0,1:T(8,128)(2,1)}), bf16[3072,256]{0,1:T(8,128)(2,1)}) %all-gather.2.cloned.1.call-update) | async-done | bytes 1572880 | tf_op jit(solution)/shard_map/all_gather | solution.py:18
  48.7 6.9 %fusion.56 = f32[2048,256]{0,1:T(8,128)S(1)} fusion(bf16[2048,3072]{1,0:T(8,128)(2,1)} %param.5, bf16[3072,256]{0,1:T(8,128)(2,1)} %all-gather.2.cloned.1.call-done), kind=kOutput, calls=%fused_computation.37 | convolution fusion | flops 3221225472 | bytes 16252928 | tf_op jit(solution)/shard_map/dot_general | solution.py:16
  55.6 50.4 %all_to_all.19 = f32[2048,4,64]{0,2,1:T(8,128)S(1)} all-to-all(f32[2048,4,64]{0,2,1:T(8,128)S(1)} %bitcast.41), channel_id=1, replica_groups=mesh['blk'=8,'slab'=4] {'slab'}, dimensions={1} | all-to-all | bytes 4194304 | tf_op jit(solution)/shard_map/all_to_all | solution.py:21
  106.0 0.0 copy-start.2
  106.0 1.5 copy.7
  107.5 0.0 reduce-scatter.2.cloned.1.call-update
  107.6 40.6 %reduce-scatter.2.cloned.1.call-done = f32[1024,64]{0,1:T(8,128)} async-done(((f32[8192,64]{0,1:T(8,128)}), f32[1024,64]{0,1:T(8,128)}) %reduce-scatter.2.cloned.1.call-update) | async-done | bytes 262160 | tf_op jit(solution)/shard_map/reduce_scatter | solution.py:23
  148.2 0.0 copy-done.2
  148.2 0.0 copy-start.3
  148.2 3.7 %fusion.6 = f32[2048,64]{0,1:T(8,128)S(1)} fusion(bf16[2048,1024]{1,0:T(8,128)(2,1)} %param.8, pred[]{:T(512)S(6)} %eq.19, f32[1024,64]{0,1:T(8,128)} %reduce-scatter.2.cloned.1.call-done, bf16[1024,64]{0,1:T(8,128)(2,1)S(1)} %copy-done.2), kind=kOutput, calls=%fused_computation.10 | convolution fusion | flops 268763136 | bytes 5111809 | tf_op jit(solution)/shard_map/dot_general | solution.py:28
  151.9 29.6 %all-reduce.4 = bf16[2048,64]{0,1:T(8,128)(2,1)S(1)} all-reduce(f32[2048,64]{0,1:T(8,128)S(1)} %fusion.6), channel_id=1, replica_groups=mesh['blk'=8,'slab'=4] {'blk'}, use_global_device_ids=true, to_apply=%region_1.2 | all-reduce | flops 131072 | bytes 786432 | tf_op jit(solution)/shard_map/psum | solution.py:30
  181.5 0.0 copy-done.3
  181.5 0.0 copy-start
  181.5 3.7 %fusion.16 = f32[1024,64]{0,1:T(8,128)S(1)} fusion(f32[1024,64]{0,1:T(8,128)S(1)} %copy-done.3, bf16[2048,64]{0,1:T(8,128)(2,1)S(1)} %all-reduce.4, bf16[1024,8192]{1,0:T(8,128)(2,1)} %param.7, pred[]{:T(512)S(6)} %gt.9), kind=kOutput, calls=%fused_computation.16 | convolution fusion | flops 268566528 | bytes 4980737 | tf_op jit(solution)/shard_map/dot_general | solution.py:35
  185.3 0.0 copy-done
  185.3 1.4 fusion.7
  186.7 29.4 %all-reduce.5 = bf16[2048,64]{0,1:T(8,128)(2,1)S(1)} all-reduce(f32[2048,64]{0,1:T(8,128)S(1)} %fusion.7), channel_id=1, replica_groups=mesh['blk'=8,'slab'=4] {'blk'}, use_global_device_ids=true, to_apply=%region_2.3 | all-reduce | flops 131072 | bytes 786432 | tf_op jit(solution)/shard_map/psum | solution.py:30
  216.1 0.0 copy-start.1
  216.1 3.7 %fusion.25 = f32[1024,64]{0,1:T(8,128)S(1)} fusion(f32[1024,64]{0,1:T(8,128)S(1)} %fusion.16, bf16[2048,64]{0,1:T(8,128)(2,1)S(1)} %all-reduce.5, bf16[1024,8192]{1,0:T(8,128)(2,1)} %param.7, pred[]{:T(512)S(6)} %gt.10), kind=kOutput, calls=%fused_computation.19 | convolution fusion | flops 268566528 | bytes 4980737 | tf_op jit(solution)/shard_map/dot_general | solution.py:35
  219.8 0.0 copy-done.1
  219.8 1.4 fusion.8
  221.2 28.8 %all-reduce.6 = bf16[2048,64]{0,1:T(8,128)(2,1)S(1)} all-reduce(f32[2048,64]{0,1:T(8,128)S(1)} %fusion.8), channel_id=1, replica_groups=mesh['blk'=8,'slab'=4] {'blk'}, use_global_device_ids=true, to_apply=%region_3.4 | all-reduce | flops 131072 | bytes 786432 | tf_op jit(solution)/shard_map/psum | solution.py:30
  250.0 6.2 %fusion.9 = f32[2048,64]{0,1:T(8,128)S(1)} fusion(bf16[2048,1024]{1,0:T(8,128)(2,1)} %param.8, f32[1024,64]{0,1:T(8,128)S(1)} %fusion.25, bf16[2048,64]{0,1:T(8,128)(2,1)S(1)} %all-reduce.6, bf16[1024,8192]{1,0:T(8,128)(2,1)} %param.7, bf16[1024,64]{0,1:T(8,128)(2,1)S(1)} %copy-done.2, pred[]{:T(512)S(6)} %eq.18, pred[]{:T(512)S(6)} %gt.11), kind=kOutput, calls=%fused_computation.13 | convolution fusion | flops 537329664 | bytes 9568258 | tf_op jit(solution)/shard_map/dot_general | solution.py:28
  256.2 28.8 %all-reduce.7 = bf16[2048,64]{0,1:T(8,128)(2,1)S(1)} all-reduce(f32[2048,64]{0,1:T(8,128)S(1)} %fusion.9), channel_id=1, replica_groups=mesh['blk'=8,'slab'=4] {'blk'}, use_global_device_ids=true, to_apply=%region_4.5 | all-reduce | flops 131072 | bytes 786432 | tf_op jit(solution)/shard_map/psum | solution.py:30
  284.9 0.7 fusion.49
Async XLA Ops:
  6.5 42.1 %all-gather.2.cloned.1.call-start = ((), (), s32[]{:S(2)}) async-start(), calls=%async_computation.2 | async-start | bytes 1966080 | tf_op jit(solution)/shard_map/all_gather | solution.py:18
  7.3 140.9 %reduce-scatter.2.cloned.1.call-start = ((), (), s32[]{:S(2)}) async-start(), calls=%async_computation.3 | async-start | bytes 2359296 | tf_op jit(solution)/shard_map/reduce_scatter | solution.py:23
  106.0 42.2 %copy-start.2 = (bf16[1024,64]{0,1:T(8,128)(2,1)S(1)}, bf16[1024,64]{0,1:T(8,128)(2,1)}, u32[]{:S(2)}) copy-start(bf16[1024,64]{0,1:T(8,128)(2,1)} %param.9) | copy-start | bytes 393220
  148.2 33.3 %copy-start.3 = (f32[1024,64]{0,1:T(8,128)S(1)}, f32[1024,64]{0,1:T(8,128)}, u32[]{:S(2)}) copy-start(f32[1024,64]{0,1:T(8,128)} %reduce-scatter.2.cloned.1.call-done) | copy-start | bytes 786436
  181.5 3.7 %copy-start = (bf16[2048,1024]{1,0:T(8,128)(2,1)S(1)}, bf16[2048,1024]{1,0:T(8,128)(2,1)}, u32[]{:S(2)}) copy-start(bf16[2048,1024]{1,0:T(8,128)(2,1)} %param.8) | copy-start | bytes 12582916
  216.1 3.7 %copy-start.1 = (bf16[2048,1024]{1,0:T(8,128)(2,1)S(1)}, bf16[2048,1024]{1,0:T(8,128)(2,1)}, u32[]{:S(2)}) copy-start(bf16[2048,1024]{1,0:T(8,128)(2,1)} %param.8) | copy-start | bytes 12582916
Sparse Core Ops, SparseCore 0:
  8.9 39.7 all-gather.1
  107.7 40.4 reduce-scatter.1
where the time goes:
time: 293 us
  blocking collectives  167 us (57%)
  waiting for transfers between devices  82.7 us (28%)
  matrix products  27 us (9%)
  between operations  13.5 us (5%)
    psum x4, blocking collectives, body(): newest = lax.psum(term, 'blk').astype(jnp.bfloat16)  117 us
    all_to_all x1, blocking collectives, body(): lax.all_to_all(partial_value, 'slab', split_axis=1, concat_axis=0, tiled=...  50.4 us
    all_gather x1, waiting for transfers between devices, body(): lax.all_gather(solved, 'slab', axis=1, tiled=True)  41.4 us
    reduce_scatter x1, waiting for transfers between devices, body(): lax.psum_scatter(window_terms, 'blk', scatter_dimension=0, tiled=True)  40.6 us
    dot_general x4, matrix products, body(): term = jnp.dot(inv_diag, resid, preferred_element_type=jnp.float32)  12.6 us
    dot_general x2, matrix products, body(): update = jnp.dot(columns, newest, preferred_element_type=jnp.float32)  7.47 us
    dot_general x1, matrix products, body(): jnp.dot(old_factor, lax.all_gather(solved, 'slab', axis=1, tiled=True), p...  6.89 us
  transfers between devices with their start and end apart: 2, of which 2 were waited for; matrix products, arithmetic and copies ran while one was open for 0% of the time, Pallas kernels for 0%

commit v1 on v0

--- a/solution.py
+++ b/solution.py
@@ -4,6 +4,18 @@
 from jax.sharding import PartitionSpec as P
 
 STEPS = 4
+
+
+def keep_up_the_results(field_in):
+    r1, kept_arr = (lax.axis_size("slab"), lax.axis_index("slab"))
+    f_now, carry = (field_in, 1)
+    while carry < r1:
+        x_next = lax.ppermute(f_now, "slab", tuple(((no, no ^ carry) for no in range(r1))))
+        r_now = jnp.concatenate([f_now, x_next], axis=1)
+        base_arr = jnp.concatenate([x_next, f_now], axis=1)
+        f_now = jnp.where(kept_arr & carry == 0, r_now, base_arr)
+        carry = 2 * carry
+    return f_now
 
 
 def body(old_factor, solved, band, inv_diag, rhs):
@@ -14,9 +26,7 @@
     own_block = own_index // group_size
     offset = own_index % group_size * own_rows
     partial_value = jnp.dot(
-        old_factor,
-        lax.all_gather(solved, "slab", axis=1, tiled=True),
-        preferred_element_type=jnp.float32,
+        old_factor, keep_up_the_results(solved), preferred_element_type=jnp.float32
     )
     window_terms = lax.all_to_all(partial_value, "slab", split_axis=1, concat_axis=0, tiled=True)
     source = rhs.astype(jnp.float32)

time: 293 us -> 302 us (1.031)
  starting transfers between devices: 0.04 us -> 5.88 us
    ppermute x0 -> x2, waiting for transfers between devices: none -> 43 us  [keep_up_the_results(): lax.ppermute(f_now, 'slab', tuple(((no, no ^ carry) for no in range(r1))))]
    all_gather x1 -> x0, waiting for transfers between devices: 41.4 us -> none  [body(): lax.all_gather(solved, 'slab', axis=1, tiled=True)]
    ppermute x0 -> x2, starting transfers between devices: none -> 5.87 us  [keep_up_the_results(): lax.ppermute(f_now, 'slab', tuple(((no, no ^ carry) for no in range(r1))))]
  transfers between devices with their start and end apart: 2 -> 3, of which waited for: 2 -> 3; matrix products, arithmetic and copies ran while one was open for 0% -> 0% of each run, Pallas kernels for 0% -> 0%
where the time goes in v1:
time: 302 us
  blocking collectives  169 us (56%)
  waiting for transfers between devices  83.4 us (28%)
  matrix products  26.6 us (9%)
  between operations  13.5 us (4%)
  starting transfers between devices  5.88 us (2%)
    psum x4, blocking collectives, body(): newest = lax.psum(term, 'blk').astype(jnp.bfloat16)  116 us
    all_to_all x1, blocking collectives, body(): lax.all_to_all(partial_value, 'slab', split_axis=1, concat_axis=0, tiled=...  52.8 us
    ppermute x2, waiting for transfers between devices, keep_up_the_results(): lax.ppermute(f_now, 'slab', tuple(((no, no ^ carry) for no in range(r1))))  43 us
    reduce_scatter x1, waiting for transfers between devices, body(): lax.psum_scatter(window_terms, 'blk', scatter_dimension=0, tiled=True)  40.3 us
    dot_general x4, matrix products, body(): term = jnp.dot(inv_diag, resid, preferred_element_type=jnp.float32)  12.6 us
    dot_general x2, matrix products, body(): update = jnp.dot(columns, newest, preferred_element_type=jnp.float32)  7.47 us
    dot_general x1, matrix products, body(): jnp.dot(old_factor, keep_up_the_results(solved), preferred_element_type=j...  6.46 us
  transfers between devices with their start and end apart: 3, of which 3 were waited for; matrix products, arithmetic and copies ran while one was open for 0% of the time, Pallas kernels for 0%

profile of v1, /device:TPU:0, one launch (start us, length us, event | category | flops | bytes accessed | tf_op | source)
XLA Modules:
  0.0 302.1 jit_solution(4494129183030168565)
XLA Ops:
  6.5 0.0 reduce-scatter.2.cloned.1.call-start
  6.5 3.1 %collective-permute-start = (bf16[3072,64]{0,1:T(8,128)(2,1)}, bf16[3072,64]{0,1:T(8,128)(2,1)S(1)}, u32[]{:S(2)}, u32[]{:S(2)}) collective-permute-start(bf16[3072,64]{0,1:T(8,128)(2,1)} %param.6), channel_id=1, source_target_pairs={{0,1},{1,0},{2,3},{3,2},{4,5},{5,4},{6,7},{7,6},{8,9},{9,8},{10,11... | collective-permute-start | bytes 1179656 | tf_op jit(solution)/shard_map/ppermute | solution.py:13
  9.6 9.3 %collective-permute-done = bf16[3072,64]{0,1:T(8,128)(2,1)S(1)} collective-permute-done((bf16[3072,64]{0,1:T(8,128)(2,1)}, bf16[3072,64]{0,1:T(8,128)(2,1)S(1)}, u32[]{:S(2)}, u32[]{:S(2)}) %collective-permute-start) | collective-permute-done | bytes 393248 | tf_op jit(solution)/shard_map/ppermute | solution.py:13
  18.9 1.3 maximum_select_fusion.2
  20.3 2.8 collective-permute-start.1
  23.1 33.7 %collective-permute-done.1 = bf16[3072,128]{0,1:T(8,128)(2,1)S(1)} collective-permute-done((bf16[3072,128]{0,1:T(8,128)(2,1)S(1)}, bf16[3072,128]{0,1:T(8,128)(2,1)S(1)}, u32[]{:S(2)}, u32[]{:S(2)}) %collective-permute-start.1) | collective-permute-done | bytes 786464 | tf_op jit(solution)/shard_map/ppermute | solution.py:13
  56.8 6.5 %fusion.10 = f32[256,2048]{1,0:T(8,128)S(1)} fusion(bf16[2048,3072]{1,0:T(8,128)(2,1)} %param.5, bf16[3072,128]{0,1:T(8,128)(2,1)S(1)} %collective-permute-done.1, bf16[3072,128]{0,1:T(8,128)(2,1)S(1)} %maximum_select_fusion.2, pred[]{:T(512)S(6)} %eq.25), kind=kOutput, calls=%fused_computation.15 | convolution fusion | flops 3228303360 | bytes 16252929 | tf_op jit(solution)/shard_map/dot_general | solution.py:28
  63.2 52.8 %all_to_all.19 = f32[2048,4,64]{0,2,1:T(8,128)S(1)} all-to-all(f32[2048,4,64]{0,2,1:T(8,128)S(1)} %bitcast.42), channel_id=1, replica_groups=mesh['blk'=8,'slab'=4] {'slab'}, dimensions={1} | all-to-all | bytes 4194304 | tf_op jit(solution)/shard_map/all_to_all | solution.py:31
  116.1 0.0 copy-start.2
  116.1 1.5 copy.7
  117.6 0.0 reduce-scatter.2.cloned.1.call-update
  117.6 40.3 %reduce-scatter.2.cloned.1.call-done = f32[1024,64]{0,1:T(8,128)} async-done(((f32[8192,64]{0,1:T(8,128)}), f32[1024,64]{0,1:T(8,128)}) %reduce-scatter.2.cloned.1.call-update) | async-done | bytes 262160 | tf_op jit(solution)/shard_map/reduce_scatter | solution.py:33
  158.0 0.0 copy-done.2
  158.0 0.0 copy-start.3
  158.0 3.7 %fusion.6 = f32[2048,64]{0,1:T(8,128)S(1)} fusion(bf16[2048,1024]{1,0:T(8,128)(2,1)} %param.8, pred[]{:T(512)S(6)} %eq.27, f32[1024,64]{0,1:T(8,128)} %reduce-scatter.2.cloned.1.call-done, bf16[1024,64]{0,1:T(8,128)(2,1)S(1)} %copy-done.2), kind=kOutput, calls=%fused_computation.10 | convolution fusion | flops 268763136 | bytes 5111809 | tf_op jit(solution)/shard_map/dot_general | solution.py:38
  161.7 29.6 %all-reduce.4 = bf16[2048,64]{0,1:T(8,128)(2,1)S(1)} all-reduce(f32[2048,64]{0,1:T(8,128)S(1)} %fusion.6), channel_id=1, replica_groups=mesh['blk'=8,'slab'=4] {'blk'}, use_global_device_ids=true, to_apply=%region_1.2 | all-reduce | flops 131072 | bytes 786432 | tf_op jit(solution)/shard_map/psum | solution.py:40
  191.3 0.0 copy-done.3
  191.3 0.0 copy-start
  191.3 3.7 %fusion.23 = f32[1024,64]{0,1:T(8,128)S(1)} fusion(f32[1024,64]{0,1:T(8,128)S(1)} %copy-done.3, bf16[2048,64]{0,1:T(8,128)(2,1)S(1)} %all-reduce.4, bf16[1024,8192]{1,0:T(8,128)(2,1)} %param.7, pred[]{:T(512)S(6)} %gt.9), kind=kOutput, calls=%fused_computation.24 | convolution fusion | flops 268566528 | bytes 4980737 | tf_op jit(solution)/shard_map/dot_general | solution.py:45
  195.1 0.0 copy-done
  195.1 1.4 fusion.7
  196.5 29.2 %all-reduce.5 = bf16[2048,64]{0,1:T(8,128)(2,1)S(1)} all-reduce(f32[2048,64]{0,1:T(8,128)S(1)} %fusion.7), channel_id=1, replica_groups=mesh['blk'=8,'slab'=4] {'blk'}, use_global_device_ids=true, to_apply=%region_2.3 | all-reduce | flops 131072 | bytes 786432 | tf_op jit(solution)/shard_map/psum | solution.py:40
  225.7 0.0 copy-start.1
  225.7 3.7 %fusion.32 = f32[1024,64]{0,1:T(8,128)S(1)} fusion(f32[1024,64]{0,1:T(8,128)S(1)} %fusion.23, bf16[2048,64]{0,1:T(8,128)(2,1)S(1)} %all-reduce.5, bf16[1024,8192]{1,0:T(8,128)(2,1)} %param.7, pred[]{:T(512)S(6)} %gt.10), kind=kOutput, calls=%fused_computation.27 | convolution fusion | flops 268566528 | bytes 4980737 | tf_op jit(solution)/shard_map/dot_general | solution.py:45
  229.4 0.0 copy-done.1
  229.4 1.4 fusion.8
  230.8 28.8 %all-reduce.6 = bf16[2048,64]{0,1:T(8,128)(2,1)S(1)} all-reduce(f32[2048,64]{0,1:T(8,128)S(1)} %fusion.8), channel_id=1, replica_groups=mesh['blk'=8,'slab'=4] {'blk'}, use_global_device_ids=true, to_apply=%region_3.4 | all-reduce | flops 131072 | bytes 786432 | tf_op jit(solution)/shard_map/psum | solution.py:40
  259.6 6.2 %fusion.9 = f32[2048,64]{0,1:T(8,128)S(1)} fusion(bf16[2048,1024]{1,0:T(8,128)(2,1)} %param.8, f32[1024,64]{0,1:T(8,128)S(1)} %fusion.32, bf16[2048,64]{0,1:T(8,128)(2,1)S(1)} %all-reduce.6, bf16[1024,8192]{1,0:T(8,128)(2,1)} %param.7, bf16[1024,64]{0,1:T(8,128)(2,1)S(1)} %copy-done.2, pred[]{:T(512)S(6)} %eq.24, pred[]{:T(512)S(6)} %gt.11), kind=kOutput, calls=%fused_computation.13 | convolution fusion | flops 537329664 | bytes 9568258 | tf_op jit(solution)/shard_map/dot_general | solution.py:38
  265.8 28.8 %all-reduce.7 = bf16[2048,64]{0,1:T(8,128)(2,1)S(1)} all-reduce(f32[2048,64]{0,1:T(8,128)S(1)} %fusion.9), channel_id=1, replica_groups=mesh['blk'=8,'slab'=4] {'blk'}, use_global_device_ids=true, to_apply=%region_4.5 | all-reduce | flops 131072 | bytes 786432 | tf_op jit(solution)/shard_map/psum | solution.py:40
  294.5 0.7 fusion.56
Async XLA Ops:
  6.5 151.4 %reduce-scatter.2.cloned.1.call-start = ((), (), s32[]{:S(2)}) async-start(), calls=%async_computation.2 | async-start | bytes 2359296 | tf_op jit(solution)/shard_map/reduce_scatter | solution.py:33
  6.5 12.4 %collective-permute-start = (bf16[3072,64]{0,1:T(8,128)(2,1)}, bf16[3072,64]{0,1:T(8,128)(2,1)S(1)}, u32[]{:S(2)}, u32[]{:S(2)}) collective-permute-start(bf16[3072,64]{0,1:T(8,128)(2,1)} %param.6), channel_id=1, source_target_pairs={{0,1},{1,0},{2,3},{3,2},{4,5},{5,4},{6,7},{7,6},{8,9},{9,8},{10,11... | collective-permute-start | bytes 1179656 | tf_op jit(solution)/shard_map/ppermute | solution.py:13
  20.3 36.5 %collective-permute-start.1 = (bf16[3072,128]{0,1:T(8,128)(2,1)S(1)}, bf16[3072,128]{0,1:T(8,128)(2,1)S(1)}, u32[]{:S(2)}, u32[]{:S(2)}) collective-permute-start(bf16[3072,128]{0,1:T(8,128)(2,1)S(1)} %maximum_select_fusion.2), channel_id=1, source_target_pairs={{0,2},{1,3},{2,0},{3,1},{4,6},{5,7},{6,4},{7,5},{8,10},{9,11},{10,... | collective-permute-start | bytes 2359304 | tf_op jit(solution)/shard_map/ppermute | solution.py:13
  116.1 41.9 %copy-start.2 = (bf16[1024,64]{0,1:T(8,128)(2,1)S(1)}, bf16[1024,64]{0,1:T(8,128)(2,1)}, u32[]{:S(2)}) copy-start(bf16[1024,64]{0,1:T(8,128)(2,1)} %param.9) | copy-start | bytes 393220
  158.0 33.4 %copy-start.3 = (f32[1024,64]{0,1:T(8,128)S(1)}, f32[1024,64]{0,1:T(8,128)}, u32[]{:S(2)}) copy-start(f32[1024,64]{0,1:T(8,128)} %reduce-scatter.2.cloned.1.call-done) | copy-start | bytes 786436
  191.3 3.7 %copy-start = (bf16[2048,1024]{1,0:T(8,128)(2,1)S(1)}, bf16[2048,1024]{1,0:T(8,128)(2,1)}, u32[]{:S(2)}) copy-start(bf16[2048,1024]{1,0:T(8,128)(2,1)} %param.8) | copy-start | bytes 12582916
  225.7 3.8 %copy-start.1 = (bf16[2048,1024]{1,0:T(8,128)(2,1)S(1)}, bf16[2048,1024]{1,0:T(8,128)(2,1)}, u32[]{:S(2)}) copy-start(bf16[2048,1024]{1,0:T(8,128)(2,1)} %param.8) | copy-start | bytes 12582916
Sparse Core Ops, SparseCore 0:
  117.7 40.1 reduce-scatter.1
